TPU v7x, 32 devices: a whole 2x2x4 slice. The times are simulated.
32 devices in a mesh: row: 8 (over z, y), col: 4 (over x, core).
Axes of the slice: x: 2, y: 2, z: 4, core: 2. Of those that a mesh axis runs over, the one named last changes fastest.
Arguments:
- left_blocks: bfloat16 [2, 128, 512, 128], P(None, 'row', 'col'), may hold values from -0.1875 to 0.1875
- right_blocks: bfloat16 [128, 512, 128], P('row', 'col'), may hold values from -6 to 6
- left_index: int32 [2, 512, 32], P(None, 'row', 'col'), may hold values from 0 to 16, as said below
- right_index: int32 [2, 512, 32], P(None, 'row', 'col'), may hold values from 0 to 15
Outputs:
- out_blocks: bfloat16 [512, 512, 128], P('row', 'col')
Inputs may be any that keep to these rules, and one draw needn't show every extreme that they name: `left_index`: the value 16 marks a padded pair that adds nothing; in every step and on every device each result block has 1 to 8 live pairs.
All inputs are finite; a program needn't handle non-finite values.
Results may differ from a plain program's by a relative error of at most 0.001.
Values may be sent and summed in bfloat16 or wider, within the bound.
No kernel may reach another device: no remote copies, remote signals or barrier semaphores. Data moves between devices by JAX's collectives and lax.ppermute only.
A program may use at most 128 MiB of HBM per device.

v0:
```python
import functools

import jax
import jax.numpy as jnp
from jax import lax
from jax.experimental import pallas as pl
from jax.experimental.pallas import tpu as pltpu
from jax.sharding import PartitionSpec as P


VMEM = pl.BlockSpec(memory_space=pltpu.VMEM)
SMEM = pl.BlockSpec(memory_space=pltpu.SMEM)
HBM = pl.BlockSpec(memory_space=pltpu.HBM)


def in_vmem(x):
    return pltpu.with_memory_space_constraint(x, pltpu.VMEM)


def holders(row, col_count, ahead, bit):
    held = {(row + ahead) % col_count}
    step = col_count // 2
    while step > bit:
        held |= {c ^ step for c in held}
        step //= 2
    return held


def full_pairs(row_count, col_count, wanted):
    pairs = []
    for row in range(row_count):
        pair_of = dict(wanted(row))
        sources = [c for c in range(col_count) if c not in pair_of]
        targets = set(range(col_count)) - set(pair_of.values())
        for c in list(sources):
            if c ^ 1 in targets:
                pair_of[c] = c ^ 1
                targets.remove(c ^ 1)
                sources.remove(c)
        pair_of.update(zip(sources, sorted(targets)))
        pairs += [(row * col_count + c, row * col_count + to) for c, to in sorted(pair_of.items())]
    return pairs


def place():
    row, col = lax.axis_index("row"), lax.axis_index("col")
    ahead = (row + col) % 2
    away = col ^ ((row + ahead) % lax.axis_size("col"))
    return row % 2, ahead, away


def fetch_kernel(left, right, out, right_out, sem):
    row_count, col_count = lax.axis_size("row"), lax.axis_size("col")
    row = lax.axis_index("row")
    ahead = (row + lax.axis_index("col")) % 2
    slot = ((row + ahead) % row_count) // col_count
    copies = [
        pltpu.make_async_copy(left.at[slot], out, sem.at[0]),
        pltpu.make_async_copy(right, right_out, sem.at[1]),
    ]
    for copy in copies:
        copy.start()
    for copy in copies:
        copy.wait()


def fetch(left_blocks, right_blocks):
    return pl.pallas_call(
        fetch_kernel,
        out_shape=(
            jax.ShapeDtypeStruct(left_blocks.shape[1:], left_blocks.dtype),
            jax.ShapeDtypeStruct(right_blocks.shape, right_blocks.dtype),
        ),
        in_specs=[HBM, HBM],
        out_specs=(VMEM, VMEM),
        scratch_shapes=[pltpu.SemaphoreType.DMA((2,))],
        compiler_params=pltpu.CompilerParams(vmem_limit_bytes=4 << 20),
        name="fetch",
    )(
        pltpu.with_memory_space_constraint(left_blocks, pltpu.HBM),
        pltpu.with_memory_space_constraint(right_blocks, pltpu.HBM),
    )


def merge_kernel(bit, split, base, received, current, kept):
    odd, ahead, away = place()
    take = (away & bit) != 0
    if split:
        take = jnp.logical_and(take, jnp.logical_or(odd == 1, ahead == 0))

    @pl.when(take)
    def _():
        current[...] = received[...]

    @pl.when(jnp.logical_not(take))
    def _():
        current[...] = base[...]

    kept[...] = base[...]


def merge(bit, split, base, received):
    shape = jax.ShapeDtypeStruct(base.shape, base.dtype)
    return pl.pallas_call(
        functools.partial(merge_kernel, bit, split),
        out_shape=(shape, shape),
        in_specs=[VMEM, VMEM],
        out_specs=(VMEM, VMEM),
        compiler_params=pltpu.CompilerParams(vmem_limit_bytes=4 << 20),
        name="merge",
    )(in_vmem(base), in_vmem(received))


def products(panel, right, out):
    stored, block, _ = panel.shape
    rows = panel[...].reshape(stored * block, block)

    def one(q, carry):
        pair = jnp.concatenate([right[2 * q], right[2 * q + 1]], axis=1)
        x = jnp.dot(rows, pair, preferred_element_type=jnp.float32)
        base = 2 * q * stored
        out[pl.ds(base, stored)] = x[:, :block].reshape(stored, block, block)
        out[pl.ds(base + stored, stored)] = x[:, block:].reshape(stored, block, block)
        return carry

    lax.fori_loop(0, right.shape[0] // 2, one, 0, unroll=8)


def gathered(index, step, t, table):
    x = table[index[step, 0, t]]
    for g in range(1, index.shape[1]):
        x = x + table[index[step, g, t]]
    return x


def first_products_kernel(current, other, right, out, panel):
    _, ahead, _ = place()

    @pl.when(ahead == 0)
    def _():
        panel[...] = current[...]

    @pl.when(ahead == 1)
    def _():
        panel[...] = other[...]

    products(panel, right, out)
    out[out.shape[0] - 1] = jnp.zeros(out.shape[1:], out.dtype)


def first_sums_kernel(index, table, out):
    def one(t, carry):
        out[t] = gathered(index, 0, t, table)
        return carry

    lax.fori_loop(0, out.shape[0], one, 0, unroll=8)


def second_kernel(per_block, index, current, other, crossed, passed, right, summed, out, panel, table):
    @pl.when(pl.program_id(0) == 0)
    def _():
        odd, ahead, away = place()
        late = jnp.logical_and(odd == 0, (away & 2) != 0)
        prompt = jnp.logical_not(late)

        @pl.when(jnp.logical_and(late, ahead == 0))
        def _():
            panel[...] = passed[...]

        @pl.when(jnp.logical_and(late, ahead == 1))
        def _():
            panel[...] = crossed[...]

        @pl.when(jnp.logical_and(prompt, ahead == 0))
        def _():
            panel[...] = other[...]

        @pl.when(jnp.logical_and(prompt, ahead == 1))
        def _():
            panel[...] = current[...]

        products(panel, right, table)
        table[table.shape[0] - 1] = jnp.zeros(table.shape[1:], table.dtype)

    base = pl.program_id(0) * per_block

    def one(j, carry):
        t = base + j
        out[j] = (summed[t] + gathered(index, 1, t, table)).astype(out.dtype)
        return carry

    lax.fori_loop(0, per_block, one, 0, unroll=8)


def cost(flops, bytes_accessed):
    return pl.CostEstimate(flops=flops, bytes_accessed=bytes_accessed, transcendentals=0)


def both_steps(left_blocks, right_blocks, left_index, right_index):
    row_count, col_count = lax.axis_size("row"), lax.axis_size("col")
    stored, block, _ = right_blocks.shape
    slots = left_index.shape[1]
    entries = stored * stored + 1
    both = ("row", "col")

    moved_right = lax.ppermute(
        right_blocks, "row", [(r, (r - 1) % row_count) for r in range(row_count)]
    )
    left_at, right_at = left_index.transpose(0, 2, 1), right_index.transpose(0, 2, 1)
    index = jnp.where(left_at < stored, right_at * stored + left_at, stored * stored)

    base, own_right = fetch(left_blocks, right_blocks)
    bit = col_count // 2
    while bit > 2:
        pairs = full_pairs(row_count, col_count, lambda row: [
            (c, c ^ bit) for c in holders(row, col_count, 0, bit) | holders(row, col_count, 1, bit)
        ])
        base, _ = merge(bit, False, base, lax.ppermute(base, both, pairs))
        bit //= 2
    early = full_pairs(row_count, col_count, lambda row: [
        (c, c ^ 2)
        for ahead in range(1 + row % 2)
        for c in holders(row, col_count, ahead, 2)
    ])
    late = full_pairs(row_count, col_count, lambda row: [
        (c, c ^ 2) for c in holders(row, col_count, 1, 2) if row % 2 == 0
    ])
    across = [(c, c ^ 1) for c in range(col_count)]
    received = lax.ppermute(base, both, early)
    current, kept = merge(2, True, base, received)
    crossed = lax.ppermute(kept, both, late)
    other = lax.ppermute(current, "col", across)
    passed = lax.ppermute(crossed, "col", across)

    flops = 4 * stored * stored * block**3
    table = pl.pallas_call(
        first_products_kernel,
        out_shape=jax.ShapeDtypeStruct((entries, block, block), jnp.float32),
        in_specs=[VMEM] * 3,
        out_specs=VMEM,
        scratch_shapes=[pltpu.VMEM(right_blocks.shape, right_blocks.dtype)],
        compiler_params=pltpu.CompilerParams(vmem_limit_bytes=22 << 20),
        cost_estimate=cost(flops, 4 << 20),
        name="products",
    )(in_vmem(current), in_vmem(other), in_vmem(own_right))
    summed = pl.pallas_call(
        first_sums_kernel,
        out_shape=jax.ShapeDtypeStruct((slots, block, block), jnp.float32),
        in_specs=[SMEM, VMEM],
        out_specs=VMEM,
        compiler_params=pltpu.CompilerParams(vmem_limit_bytes=8 << 20),
        cost_estimate=cost(flops, 4 << 20),
        name="sums",
    )(index, in_vmem(table))
    per_block = min(slots, 16)
    return pl.pallas_call(
        functools.partial(second_kernel, per_block),
        grid=(slots // per_block,),
        out_shape=jax.ShapeDtypeStruct((slots, block, block), jnp.bfloat16),
        in_specs=[SMEM] + [VMEM] * 6,
        out_specs=pl.BlockSpec((per_block, block, block), lambda i: (i, 0, 0)),
        scratch_shapes=[
            pltpu.VMEM(right_blocks.shape, right_blocks.dtype),
            pltpu.VMEM((entries, block, block), jnp.float32),
        ],
        compiler_params=pltpu.CompilerParams(vmem_limit_bytes=22 << 20),
        cost_estimate=cost(2 * flops, 4 << 20),
        name="second",
    )(index, *map(in_vmem, (current, other, crossed, passed, moved_right, summed)))


def solution(mesh):
    return jax.shard_map(
        both_steps,
        mesh=mesh,
        in_specs=(
            P(None, "row", "col", None),
            P("row", "col", None),
            P(None, "row", "col"),
            P(None, "row", "col"),
        ),
        out_specs=P("row", "col", None),
        check_vma=False,
    )
```

profile of v0, /device:TPU:0, one launch (start us, length us, event | category | flops | bytes accessed | tf_op | source)
XLA Modules:
  0.0 34.2 jit_solution(5919782546673478806)
XLA Ops:
  0.0 1.2 %fetch.1 = (bf16[16,128,128]{2,1,0:T(8,128)(2,1)S(1)}, bf16[16,128,128]{2,1,0:T(8,128)(2,1)S(1)}) custom-call(bf16[2,16,128,128]{3,2,1,0:T(8,128)(2,1)} %left.1, bf16[16,128,128]{2,1,0:T(8,128)(2,1)} %right.1), custom_call_target="tpu_custom_call" | custom-call | tf_op jit(solution)/shard_map/fetch/pallas_call | solution.py:68
  1.2 3.0 %collective-permute-start = (bf16[16,128,128]{2,1,0:T(8,128)(2,1)S(1)}, bf16[16,128,128]{2,1,0:T(8,128)(2,1)S(1)}, u32[]{:S(2)}, u32[]{:S(2)}) collective-permute-start(bf16[16,128,128]{2,1,0:T(8,128)(2,1)S(1)} %get-tuple-element.9.base), channel_id=1, source_target_pairs={{0,2},{1,0},{2,3},{3,1},{4,5},{5,7},{6,4},{7,6},{8,9},{9,11},{10,8... | collective-permute-start | bytes 1572872 | tf_op jit(solution)/shard_map/ppermute | solution.py:229
  4.3 6.7 %collective-permute-done.received = bf16[16,128,128]{2,1,0:T(8,128)(2,1)S(1)} collective-permute-done((bf16[16,128,128]{2,1,0:T(8,128)(2,1)S(1)}, bf16[16,128,128]{2,1,0:T(8,128)(2,1)S(1)}, u32[]{:S(2)}, u32[]{:S(2)}) %collective-permute-start) | collective-permute-done | bytes 524320 | tf_op jit(solution)/shard_map/ppermute | solution.py:229
  11.0 0.1 merge.1
  11.0 0.1 collective-permute-start.2
  11.1 0.1 collective-permute-start.1
  11.2 5.0 %collective-permute-start.4 = (bf16[16,128,128]{2,1,0:T(8,128)(2,1)}, bf16[16,128,128]{2,1,0:T(8,128)(2,1)S(1)}, u32[]{:S(2)}, u32[]{:S(2)}) collective-permute-start(bf16[16,128,128]{2,1,0:T(8,128)(2,1)} %right.1), channel_id=1, source_target_pairs={{0,28},{4,0},{8,4},{12,8},{16,12},{20,16},{24,20},{28,24},{1,29},{... | collective-permute-start | bytes 1572872 | tf_op jit(solution)/shard_map/ppermute | solution.py:206
  16.2 4.6 %collective-permute-done.2.crossed = bf16[16,128,128]{2,1,0:T(8,128)(2,1)S(1)} collective-permute-done((bf16[16,128,128]{2,1,0:T(8,128)(2,1)S(1)}, bf16[16,128,128]{2,1,0:T(8,128)(2,1)S(1)}, u32[]{:S(2)}, u32[]{:S(2)}) %collective-permute-start.2) | collective-permute-done | bytes 524320 | tf_op jit(solution)/shard_map/ppermute | solution.py:231
  20.8 0.0 collective-permute-start.3
  20.8 0.7 %select_bitcast_fusion.index = s32[2,8,64]{2,1,0:T(8,128)S(1)} fusion(s32[2,64,8]{1,2,0:T(8,128)} %param.6, s32[2,64,8]{1,2,0:T(8,128)} %param.7), kind=kLoop, calls=%fused_computation | loop fusion | flops 4096 | bytes 12288 | tf_op jit(solution)/shard_map/jit(_where)/select_n | solution.py:210
  21.5 0.0 collective-permute-done.1.other
  21.5 2.4 %products.1.table = f32[257,128,128]{2,1,0:T(8,128)S(1)} custom-call(bf16[16,128,128]{2,1,0:T(8,128)(2,1)S(1)} %get-tuple-element.10.current, bf16[16,128,128]{2,1,0:T(8,128)(2,1)S(1)} %collective-permute-done.1.other, bf16[16,128,128]{2,1,0:T(8,128)(2,1)S(1)} %get-tuple-element.12.right), custom_call_target="tpu_custom_call" | custom-call | flops 2147483648 | bytes 4194304 | tf_op jit(solution)/shard_map/products/pallas_call | solution.py:236
  23.9 2.2 %sums.1.summed = f32[64,128,128]{2,1,0:T(8,128)S(1)} custom-call(s32[2,8,64]{2,1,0:T(8,128)S(1)} %select_bitcast_fusion.index, f32[257,128,128]{2,1,0:T(8,128)S(1)} %products.1.table), custom_call_target="tpu_custom_call" | custom-call | flops 2147483648 | bytes 4194304 | tf_op jit(solution)/shard_map/sums/pallas_call | solution.py:246
  26.1 1.8 %collective-permute-done.4.right = bf16[16,128,128]{2,1,0:T(8,128)(2,1)S(1)} collective-permute-done((bf16[16,128,128]{2,1,0:T(8,128)(2,1)}, bf16[16,128,128]{2,1,0:T(8,128)(2,1)S(1)}, u32[]{:S(2)}, u32[]{:S(2)}) %collective-permute-start.4) | collective-permute-done | bytes 524320 | tf_op jit(solution)/shard_map/ppermute | solution.py:206
  27.9 0.0 collective-permute-done.3.passed
  27.9 6.3 %second.1 = bf16[64,128,128]{2,1,0:T(8,128)(2,1)} custom-call(s32[2,8,64]{2,1,0:T(8,128)S(1)} %select_bitcast_fusion.index, bf16[16,128,128]{2,1,0:T(8,128)(2,1)S(1)} %get-tuple-element.10.current, bf16[16,128,128]{2,1,0:T(8,128)(2,1)S(1)} %collective-permute-done.1.other, bf16[16,128,128]{2,1,0:T(8,128)(2,1)S(1)} %collective-permute-done.2.crossed, ...), custom_call_target="tpu_custom_call" | custom-call | flops 4294967296 | bytes 4194304 | tf_op jit(solution)/shard_map/second/pallas_call | solution.py:256
Async XLA Ops:
  1.2 9.7 %collective-permute-start = (bf16[16,128,128]{2,1,0:T(8,128)(2,1)S(1)}, bf16[16,128,128]{2,1,0:T(8,128)(2,1)S(1)}, u32[]{:S(2)}, u32[]{:S(2)}) collective-permute-start(bf16[16,128,128]{2,1,0:T(8,128)(2,1)S(1)} %get-tuple-element.9.base), channel_id=1, source_target_pairs={{0,2},{1,0},{2,3},{3,1},{4,5},{5,7},{6,4},{7,6},{8,9},{9,11},{10,8... | collective-permute-start | bytes 1572872 | tf_op jit(solution)/shard_map/ppermute | solution.py:229
  11.0 9.7 %collective-permute-start.2 = (bf16[16,128,128]{2,1,0:T(8,128)(2,1)S(1)}, bf16[16,128,128]{2,1,0:T(8,128)(2,1)S(1)}, u32[]{:S(2)}, u32[]{:S(2)}) collective-permute-start(bf16[16,128,128]{2,1,0:T(8,128)(2,1)S(1)} %get-tuple-element.11), channel_id=1, source_target_pairs={{0,1},{1,3},{2,0},{3,2},{4,5},{5,4},{6,7},{7,6},{8,10},{9,8},{10,1... | collective-permute-start | bytes 1572872 | tf_op jit(solution)/shard_map/ppermute | solution.py:231
  11.1 10.4 %collective-permute-start.1 = (bf16[16,128,128]{2,1,0:T(8,128)(2,1)S(1)}, bf16[16,128,128]{2,1,0:T(8,128)(2,1)S(1)}, u32[]{:S(2)}, u32[]{:S(2)}) collective-permute-start(bf16[16,128,128]{2,1,0:T(8,128)(2,1)S(1)} %get-tuple-element.10.current), channel_id=1, source_target_pairs={{0,1},{1,0},{2,3},{3,2},{4,5},{5,4},{6,7},{7,6},{8,9},{9,8},{10,11... | collective-permute-start | bytes 1572872 | tf_op jit(solution)/shard_map/ppermute | solution.py:232
  11.2 16.7 %collective-permute-start.4 = (bf16[16,128,128]{2,1,0:T(8,128)(2,1)}, bf16[16,128,128]{2,1,0:T(8,128)(2,1)S(1)}, u32[]{:S(2)}, u32[]{:S(2)}) collective-permute-start(bf16[16,128,128]{2,1,0:T(8,128)(2,1)} %right.1), channel_id=1, source_target_pairs={{0,28},{4,0},{8,4},{12,8},{16,12},{20,16},{24,20},{28,24},{1,29},{... | collective-permute-start | bytes 1572872 | tf_op jit(solution)/shard_map/ppermute | solution.py:206
  20.8 7.1 %collective-permute-start.3 = (bf16[16,128,128]{2,1,0:T(8,128)(2,1)S(1)}, bf16[16,128,128]{2,1,0:T(8,128)(2,1)S(1)}, u32[]{:S(2)}, u32[]{:S(2)}) collective-permute-start(bf16[16,128,128]{2,1,0:T(8,128)(2,1)S(1)} %collective-permute-done.2.crossed), channel_id=1, source_target_pairs={{0,1},{1,0},{2,3},{3,2},{4,5},{5,4},{6,7},{7,6},{8,9},{9,8},{10,11... | collective-permute-start | bytes 1572872 | tf_op jit(solution)/shard_map/ppermute | solution.py:233
where the time goes:
time: 34.4 us; the launch traced here: 34.2 us
  waiting for transfers between devices  13.1 us (38%)
  Pallas kernels  12.1 us (35%)
  starting transfers between devices  8.14 us (24%)
  other arithmetic  0.72 us (2%)
    ppermute x1, waiting for transfers between devices, both_steps(): received = lax.ppermute(base, both, early)  6.7 us
    pallas_call x1, Pallas kernels, both_steps(): pl.pallas_call(functools.partial(second_kernel, per_block), grid=(slots /...  6.26 us
    ppermute x1, starting transfers between devices, both_steps(): lax.ppermute(right_blocks, 'row', [(r, (r - 1) % row_count) for r in rang...  4.98 us
    ppermute x1, waiting for transfers between devices, both_steps(): crossed = lax.ppermute(kept, both, late)  4.62 us
    ppermute x1, starting transfers between devices, both_steps(): received = lax.ppermute(base, both, early)  3.03 us
    pallas_call x1, Pallas kernels, both_steps(): pl.pallas_call(first_products_kernel, out_shape=jax.ShapeDtypeStruct((ent...  2.37 us
    pallas_call x1, Pallas kernels, both_steps(): pl.pallas_call(first_sums_kernel, out_shape=jax.ShapeDtypeStruct((slots,...  2.2 us
    ppermute x1, waiting for transfers between devices, both_steps(): lax.ppermute(right_blocks, 'row', [(r, (r - 1) % row_count) for r in rang...  1.81 us
  transfers between devices with their start and end apart: 5, of which 3 were waited for; matrix products, arithmetic and copies ran while one was open for 2% of the time, Pallas kernels for 13%

commit v1 on v0

v1 whole, which is shorter than its diff:
```python
import functools

import jax
import jax.numpy as jnp
from jax import lax
from jax.experimental import pallas as pl
from jax.experimental.pallas import tpu as pltpu
from jax.sharding import PartitionSpec as P


VMEM = pl.BlockSpec(memory_space=pltpu.VMEM)
HBM = pl.BlockSpec(memory_space=pltpu.HBM)


def in_vmem(x):
    return pltpu.with_memory_space_constraint(x, pltpu.VMEM)


def holders(row, col_count, ahead, bit):
    held = {(row + ahead) % col_count}
    step = col_count // 2
    while step > bit:
        held |= {c ^ step for c in held}
        step //= 2
    return held


def full_pairs(row_count, col_count, wanted):
    pairs = []
    for row in range(row_count):
        pair_of = dict(wanted(row))
        sources = [c for c in range(col_count) if c not in pair_of]
        targets = set(range(col_count)) - set(pair_of.values())
        for c in list(sources):
            if c ^ 1 in targets:
                pair_of[c] = c ^ 1
                targets.remove(c ^ 1)
                sources.remove(c)
        pair_of.update(zip(sources, sorted(targets)))
        pairs += [(row * col_count + c, row * col_count + to) for c, to in sorted(pair_of.items())]
    return pairs


def place():
    row, col = lax.axis_index("row"), lax.axis_index("col")
    return row % 2, (col ^ row) % 4, (col ^ (row + 1)) % 4


def plan_step(left_at, right_at, stored):
    group, slots = left_at.shape
    dead = stored * stored
    index = jnp.where(left_at < stored, right_at * stored + left_at, dead)
    rows = [index[g : g + 1] for g in range(group)]
    for turn in range(group):
        for g in range(turn % 2, group - 1, 2):
            rows[g], rows[g + 1] = jnp.minimum(*rows[g : g + 2]), jnp.maximum(*rows[g : g + 2])
    live = sum((row < dead).astype(jnp.float32) for row in rows)
    at_row = lax.broadcasted_iota(jnp.int32, (slots, slots), 0).astype(jnp.float32)
    at_col = lax.broadcasted_iota(jnp.int32, (slots, slots), 1).astype(jnp.float32)
    slot = at_col[:1]
    key = live * slots - slot
    column = jnp.sum(jnp.where(at_row == at_col, key, 0.0), axis=1, keepdims=True)
    rank = jnp.sum((key > column).astype(jnp.float32), axis=1, keepdims=True)
    pick = (rank == at_col).astype(jnp.float32)
    data = jnp.concatenate([row.astype(jnp.float32) for row in rows] + [live, slot], axis=0)
    sorted_data = jnp.dot(
        data, pick, precision=lax.Precision.HIGHEST, preferred_element_type=jnp.float32
    )
    return (sorted_data + 0.5).astype(jnp.int32)


def fetch_kernel(left, right, left_at, right_at, own, low, high, plan, at, sem):
    row_count, col_count = lax.axis_size("row"), lax.axis_size("col")
    row = lax.axis_index("row")
    ahead = (row + lax.axis_index("col")) % 2
    slot = ((row + ahead) % row_count) // col_count
    split = low.shape[0]
    copies = [
        pltpu.make_async_copy(left_at, at.at[0], sem.at[0]),
        pltpu.make_async_copy(right_at, at.at[1], sem.at[1]),
        pltpu.make_async_copy(left.at[slot], own, sem.at[2]),
        pltpu.make_async_copy(right.at[pl.ds(0, split)], low, sem.at[3]),
        pltpu.make_async_copy(right.at[pl.ds(split, high.shape[0])], high, sem.at[4]),
    ]
    for copy in copies:
        copy.start()
    for copy in copies[:2]:
        copy.wait()
    for step in range(plan.shape[0]):
        plan[step] = plan_step(at[0, step], at[1, step], own.shape[0])
    for copy in copies[2:]:
        copy.wait()


def fetch(left_blocks, right_blocks, left_at, right_at, split):
    stored, *block = right_blocks.shape
    steps, group, slots = left_at.shape
    return pl.pallas_call(
        fetch_kernel,
        out_shape=tuple(
            jax.ShapeDtypeStruct((count, *block), right_blocks.dtype)
            for count in (stored, split, stored - split)
        ) + (jax.ShapeDtypeStruct((steps, group + 2, slots), jnp.int32),),
        in_specs=[HBM] * 4,
        out_specs=(VMEM,) * 4,
        scratch_shapes=[
            pltpu.VMEM((2, steps, group, slots), jnp.int32),
            pltpu.SemaphoreType.DMA((5,)),
        ],
        compiler_params=pltpu.CompilerParams(vmem_limit_bytes=4 << 20),
        name="fetch",
    )(*(pltpu.with_memory_space_constraint(x, pltpu.HBM)
        for x in (left_blocks, right_blocks, left_at, right_at)))


def merge_kernel(bit, base, received, out):
    row, col = lax.axis_index("row"), lax.axis_index("col")
    away = col ^ ((row + (row + col) % 2) % lax.axis_size("col"))
    take = (away & bit) != 0

    @pl.when(take)
    def _():
        out[...] = received[...]

    @pl.when(jnp.logical_not(take))
    def _():
        out[...] = base[...]


def merge(bit, base, received):
    return pl.pallas_call(
        functools.partial(merge_kernel, bit),
        out_shape=jax.ShapeDtypeStruct(base.shape, base.dtype),
        in_specs=[VMEM, VMEM],
        out_specs=VMEM,
        compiler_params=pltpu.CompilerParams(vmem_limit_bytes=4 << 20),
        name="merge",
    )(in_vmem(base), in_vmem(received))


def choose(panel, options):
    for condition, array in options:
        @pl.when(condition)
        def _():
            panel[...] = array[...]


def products(panel, right, out, first):
    stored, block, _ = panel.shape
    rows = panel[...].reshape(stored * block, block)
    for q in range(right.shape[0] // 2):
        pair = jnp.concatenate([right[2 * q], right[2 * q + 1]], axis=1)
        x = jnp.dot(rows, pair, preferred_element_type=jnp.float32)
        base = (first + 2 * q) * stored
        out[pl.ds(base, stored)] = x[:, :block].reshape(stored, block, block)
        out[pl.ds(base + stored, stored)] = x[:, block:].reshape(stored, block, block)


def add_up(plan, step, table, per_turn, put):
    group = plan.shape[1] - 2

    def turn(i, carry):
        first = i * per_turn
        most = jnp.clip(plan[step, group, first], 1, group)
        for count in range(1, group + 1):
            @pl.when(most == count)
            def _():
                for k in range(per_turn):
                    j = first + k
                    x = table[plan[step, 0, j]]
                    for g in range(1, count):
                        x = x + table[plan[step, g, j]]
                    put(plan[step, group + 1, j], x)

        return carry

    lax.fori_loop(0, plan.shape[2] // per_turn, turn, 0)


def clear_last(table):
    table[table.shape[0] - 1] = jnp.zeros(table.shape[1:], table.dtype)


def first_products_kernel(base, beside, across, passed, low, high, out, panel):
    _, d0, _ = place()
    choose(panel, [(d0 == 0, base), (d0 == 1, beside), (d0 == 2, across), (d0 == 3, passed)])
    products(panel, low, out, 0)
    products(panel, high, out, low.shape[0])
    clear_last(out)


def first_sums_kernel(per_turn, plan_in, table, out, plan, sem):
    pltpu.async_copy(plan_in, plan, sem).wait()

    def put(t, x):
        out[t] = x

    add_up(plan, 0, table, per_turn, put)


def half_products_kernel(base, beside, across, passed, across1, passed1, low, panel, table):
    odd, d0, d1 = place()
    plain = odd == 1
    choose(panel, [
        (d1 == 0, base),
        (jnp.logical_and(d1 == 1, plain) | jnp.logical_and(d0 == 0, ~plain), beside),
        (jnp.logical_and(d1 == 2, plain), across),
        (jnp.logical_and(d1 == 3, plain), passed),
        (jnp.logical_and(d0 == 2, ~plain), across1),
        (jnp.logical_and(d0 == 3, ~plain), passed1),
    ])
    products(panel, low, table, 0)
    clear_last(table)


def last_kernel(per_turn, plan_in, panel, high, summed, table_in, table, out, stage, plan, sem):
    del table_in
    planned = pltpu.make_async_copy(plan_in, plan, sem.at[0])
    planned.start()
    products(panel, high, table, panel.shape[0] - high.shape[0])
    planned.wait()

    def put(t, x):
        stage[t] = (summed[t] + x).astype(stage.dtype)
        pltpu.make_async_copy(stage.at[t], out.at[t], sem.at[1]).start()

    add_up(plan, 1, table, per_turn, put)
    pltpu.make_async_copy(stage, out, sem.at[1]).wait()


def cost(flops, bytes_accessed):
    return pl.CostEstimate(flops=flops, bytes_accessed=bytes_accessed, transcendentals=0)


def both_steps(left_blocks, right_blocks, left_index, right_index):
    row_count, col_count = lax.axis_size("row"), lax.axis_size("col")
    stored, block, _ = right_blocks.shape
    slots = left_index.shape[1]
    entries = stored * stored + 1
    both = ("row", "col")

    def permute(x, axis, pairs):
        return in_vmem(lax.ppermute(x, axis, pairs))

    left_at, right_at = left_index.transpose(0, 2, 1), right_index.transpose(0, 2, 1)
    base, low, high, plan = fetch(left_blocks, right_blocks, left_at, right_at, stored - stored // 4)
    bit = col_count // 2
    while bit > 2:
        pairs = full_pairs(row_count, col_count, lambda row: [
            (c, c ^ bit) for c in holders(row, col_count, 0, bit) | holders(row, col_count, 1, bit)
        ])
        base = merge(bit, base, lax.ppermute(base, both, pairs))
        bit //= 2
    crossing = full_pairs(row_count, col_count, lambda row: [
        (c, c ^ 2)
        for ahead in range(1 + row % 2)
        for c in holders(row, col_count, ahead, 2)
    ])
    again = full_pairs(row_count, col_count, lambda row: [
        (c, c ^ 2) for c in holders(row, col_count, 0, 2) if row % 2 == 0
    ])
    beside_pairs = [(c, c ^ 1) for c in range(col_count)]
    down = [(r, (r - 1) % row_count) for r in range(row_count)]
    base = in_vmem(base)
    across = permute(base, both, crossing)
    beside = permute(base, "col", beside_pairs)
    low1 = permute(low, "row", down)
    high1 = permute(high, "row", down)
    across1 = permute(beside, both, again)
    passed = permute(across, "col", beside_pairs)
    passed1 = permute(across1, "col", beside_pairs)

    plan = in_vmem(plan)
    per_turn = 8
    flops = 4 * stored * stored * block**3
    table_shape = jax.ShapeDtypeStruct((entries, block, block), jnp.float32)
    panel_shape = jax.ShapeDtypeStruct(base.shape, base.dtype)
    table = pl.pallas_call(
        first_products_kernel,
        out_shape=table_shape,
        in_specs=[VMEM] * 6,
        out_specs=VMEM,
        scratch_shapes=[pltpu.VMEM(base.shape, base.dtype)],
        compiler_params=pltpu.CompilerParams(vmem_limit_bytes=4 << 20),
        cost_estimate=cost(flops, 4 << 20),
        name="products",
    )(base, beside, across, passed, in_vmem(low), in_vmem(high))
    summed = pl.pallas_call(
        functools.partial(first_sums_kernel, per_turn),
        out_shape=jax.ShapeDtypeStruct((slots, block, block), jnp.float32),
        in_specs=[VMEM, VMEM],
        out_specs=VMEM,
        scratch_shapes=[pltpu.SMEM(plan.shape, plan.dtype), pltpu.SemaphoreType.DMA],
        compiler_params=pltpu.CompilerParams(vmem_limit_bytes=4 << 20),
        cost_estimate=cost(flops, 4 << 20),
        name="sums",
    )(plan, in_vmem(table))
    panel, table = pl.pallas_call(
        half_products_kernel,
        out_shape=(panel_shape, table_shape),
        in_specs=[VMEM] * 7,
        out_specs=(VMEM, VMEM),
        compiler_params=pltpu.CompilerParams(vmem_limit_bytes=4 << 20),
        cost_estimate=cost(flops // 2, 4 << 20),
        name="half",
    )(base, beside, across, passed, across1, passed1, low1)
    return pl.pallas_call(
        functools.partial(last_kernel, per_turn),
        out_shape=(table_shape, jax.ShapeDtypeStruct((slots, block, block), jnp.bfloat16)),
        in_specs=[VMEM] * 5,
        out_specs=(VMEM, HBM),
        scratch_shapes=[
            pltpu.VMEM((slots, block, block), jnp.bfloat16),
            pltpu.SMEM(plan.shape, plan.dtype),
            pltpu.SemaphoreType.DMA((2,)),
        ],
        input_output_aliases={4: 0},
        compiler_params=pltpu.CompilerParams(vmem_limit_bytes=6 << 20),
        cost_estimate=cost(2 * flops, 4 << 20),
        name="last",
    )(plan, in_vmem(panel), high1, in_vmem(summed), in_vmem(table))[1]


def solution(mesh):
    return jax.shard_map(
        both_steps,
        mesh=mesh,
        in_specs=(
            P(None, "row", "col", None),
            P("row", "col", None),
            P(None, "row", "col"),
            P(None, "row", "col"),
        ),
        out_specs=P("row", "col", None),
        check_vma=False,
    )
```

time: 34.4 us -> 36.4 us (1.058)
  starting transfers between devices: 8.14 us -> 11 us
  Pallas kernels: 12.1 us -> 10.4 us
  waiting for transfers between devices: 13.1 us -> 14.7 us
  other arithmetic: 0.72 us -> 0 us
    ppermute x5 -> x7, starting transfers between devices: 8.14 us -> 11 us  [permute(): return in_vmem(lax.ppermute(x, axis, pairs))]
    pallas_call x5, Pallas kernels: 12.1 us -> 10.4 us  [the longest x1 2.89 us: both_steps(): pl.pallas_call(functools.partial(last_kernel, per_turn), out_shape=(table...]
    ppermute x5 -> x7, waiting for transfers between devices: 13.1 us -> 14.7 us  [permute(): return in_vmem(lax.ppermute(x, axis, pairs))]
    select_n x1 -> x0, other arithmetic: 0.72 us -> none  [both_steps(): jnp.where(left_at < stored, right_at * stored + left_at, stored * stored)]
  transfers between devices with their start and end apart: 5 -> 7, of which waited for: 3 -> 3; matrix products, arithmetic and copies ran while one was open for 2% -> 0% of each run, Pallas kernels for 13% -> 17%
where the time goes in v1:
time: 36.4 us; the launch traced here: 36.2 us
  waiting for transfers between devices  14.7 us (40%)
  starting transfers between devices  11 us (30%)
  Pallas kernels  10.4 us (29%)
    ppermute x7, waiting for transfers between devices, permute(): return in_vmem(lax.ppermute(x, axis, pairs))  14.7 us
    ppermute x7, starting transfers between devices, permute(): return in_vmem(lax.ppermute(x, axis, pairs))  11 us
    pallas_call x1, Pallas kernels, both_steps(): pl.pallas_call(functools.partial(last_kernel, per_turn), out_shape=(table...  2.89 us
    pallas_call x1, Pallas kernels, both_steps(): pl.pallas_call(first_products_kernel, out_shape=table_shape, in_specs=[VM...  2.37 us
    pallas_call x1, Pallas kernels, both_steps(): pl.pallas_call(functools.partial(first_sums_kernel, per_turn), out_shape=...  2.11 us
    pallas_call x1, Pallas kernels, both_steps(): pl.pallas_call(half_products_kernel, out_shape=(panel_shape, table_shape)...  1.82 us
    pallas_call x1, Pallas kernels, fetch(): pl.pallas_call(fetch_kernel, out_shape=tuple((jax.ShapeDtypeStruct((count...  1.26 us
  transfers between devices with their start and end apart: 7, of which 3 were waited for; matrix products, arithmetic and copies ran while one was open for 0% of the time, Pallas kernels for 17%

profile of v1, /device:TPU:0, one launch (start us, length us, event | category | flops | bytes accessed | tf_op | source)
XLA Modules:
  0.0 36.2 jit_solution(11849282029415301983)
XLA Ops:
  0.0 1.3 %fetch.1 = (bf16[16,128,128]{2,1,0:T(8,128)(2,1)S(1)}, bf16[12,128,128]{2,1,0:T(8,128)(2,1)S(1)}, bf16[4,128,128]{2,1,0:T(8,128)(2,1)S(1)}, s32[2,10,64]{2,1,0:T(8,128)S(1)}) custom-call(bf16[2,16,128,128]{3,2,1,0:T(8,128)(2,1)} %left.1, bf16[16,128,128]{2,1,0:T(8,128)(2,1)} %right.1, s32[2,8,64]{2,1,0:T(8,128)} %bitcast.2, s32[2,8,64]{2,1,0:T(8,128)} %bitcast.3), custom_call_target="tpu_custom_call" | custom-call | tf_op jit(solution)/shard_map/fetch/pallas_call | solution.py:98
  1.3 0.6 %collective-permute-start = (bf16[16,128,128]{2,1,0:T(8,128)(2,1)S(1)}, bf16[16,128,128]{2,1,0:T(8,128)(2,1)S(1)}, u32[]{:S(2)}, u32[]{:S(2)}) collective-permute-start(bf16[16,128,128]{2,1,0:T(8,128)(2,1)S(1)} %get-tuple-element.13.base), channel_id=1, source_target_pairs={{0,1},{1,0},{2,3},{3,2},{4,5},{5,4},{6,7},{7,6},{8,9},{9,8},{10,11... | collective-permute-start | bytes 1572872 | tf_op jit(solution)/shard_map/ppermute | solution.py:243
  1.8 2.5 %collective-permute-start.1 = (bf16[16,128,128]{2,1,0:T(8,128)(2,1)S(1)}, bf16[16,128,128]{2,1,0:T(8,128)(2,1)S(1)}, u32[]{:S(2)}, u32[]{:S(2)}) collective-permute-start(bf16[16,128,128]{2,1,0:T(8,128)(2,1)S(1)} %get-tuple-element.13.base), channel_id=1, source_target_pairs={{0,2},{1,0},{2,3},{3,1},{4,5},{5,7},{6,4},{7,6},{8,9},{9,11},{10,8... | collective-permute-start | bytes 1572872 | tf_op jit(solution)/shard_map/ppermute | solution.py:243
  4.4 0.0 collective-permute-done.beside
  4.4 1.8 %collective-permute-start.3 = (bf16[16,128,128]{2,1,0:T(8,128)(2,1)S(1)}, bf16[16,128,128]{2,1,0:T(8,128)(2,1)S(1)}, u32[]{:S(2)}, u32[]{:S(2)}) collective-permute-start(bf16[16,128,128]{2,1,0:T(8,128)(2,1)S(1)} %collective-permute-done.beside), channel_id=1, source_target_pairs={{0,2},{1,0},{2,3},{3,1},{4,5},{5,4},{6,7},{7,6},{8,9},{9,11},{10,8... | collective-permute-start | bytes 1572872 | tf_op jit(solution)/shard_map/ppermute | solution.py:243
  6.2 4.9 %collective-permute-done.1.across = bf16[16,128,128]{2,1,0:T(8,128)(2,1)S(1)} collective-permute-done((bf16[16,128,128]{2,1,0:T(8,128)(2,1)S(1)}, bf16[16,128,128]{2,1,0:T(8,128)(2,1)S(1)}, u32[]{:S(2)}, u32[]{:S(2)}) %collective-permute-start.1) | collective-permute-done | bytes 524320 | tf_op jit(solution)/shard_map/ppermute | solution.py:243
  11.1 0.0 collective-permute-start.2
  11.1 5.6 %collective-permute-done.3.across1 = bf16[16,128,128]{2,1,0:T(8,128)(2,1)S(1)} collective-permute-done((bf16[16,128,128]{2,1,0:T(8,128)(2,1)S(1)}, bf16[16,128,128]{2,1,0:T(8,128)(2,1)S(1)}, u32[]{:S(2)}, u32[]{:S(2)}) %collective-permute-start.3) | collective-permute-done | bytes 524320 | tf_op jit(solution)/shard_map/ppermute | solution.py:243
  16.7 0.0 collective-permute-start.4
  16.7 0.0 collective-permute-start.6
  16.7 6.0 %collective-permute-start.5 = (bf16[12,128,128]{2,1,0:T(8,128)(2,1)S(1)}, bf16[12,128,128]{2,1,0:T(8,128)(2,1)S(1)}, u32[]{:S(2)}, u32[]{:S(2)}) collective-permute-start(bf16[12,128,128]{2,1,0:T(8,128)(2,1)S(1)} %get-tuple-element.14.low), channel_id=1, source_target_pairs={{0,28},{4,0},{8,4},{12,8},{16,12},{20,16},{24,20},{28,24},{1,29},{... | collective-permute-start | bytes 1179656 | tf_op jit(solution)/shard_map/ppermute | solution.py:243
  22.7 0.0 collective-permute-done.2.passed
  22.8 2.4 %products.1.table = f32[257,128,128]{2,1,0:T(8,128)S(1)} custom-call(bf16[16,128,128]{2,1,0:T(8,128)(2,1)S(1)} %get-tuple-element.13.base, bf16[16,128,128]{2,1,0:T(8,128)(2,1)S(1)} %collective-permute-done.beside, bf16[16,128,128]{2,1,0:T(8,128)(2,1)S(1)} %collective-permute-done.1.across, bf16[16,128,128]{2,1,0:T(8,128)(2,1)S(1)} %collective-permute-done.2.passed, ...), custom_call_target="tpu_custom_call" | custom-call | flops 2147483648 | bytes 4194304 | tf_op jit(solution)/shard_map/products/pallas_call | solution.py:278
  25.1 2.1 %sums.1.summed = f32[64,128,128]{2,1,0:T(8,128)S(1)} custom-call(s32[2,10,64]{2,1,0:T(8,128)S(1)} %get-tuple-element.12.plan_in, f32[257,128,128]{2,1,0:T(8,128)S(1)} %products.1.table), custom_call_target="tpu_custom_call" | custom-call | flops 2147483648 | bytes 4194304 | tf_op jit(solution)/shard_map/sums/pallas_call | solution.py:288
  27.2 4.3 %collective-permute-done.5.low = bf16[12,128,128]{2,1,0:T(8,128)(2,1)S(1)} collective-permute-done((bf16[12,128,128]{2,1,0:T(8,128)(2,1)S(1)}, bf16[12,128,128]{2,1,0:T(8,128)(2,1)S(1)}, u32[]{:S(2)}, u32[]{:S(2)}) %collective-permute-start.5) | collective-permute-done | bytes 393248 | tf_op jit(solution)/shard_map/ppermute | solution.py:243
  31.5 0.0 collective-permute-done.4.passed1
  31.5 1.8 %half.1 = (bf16[16,128,128]{2,1,0:T(8,128)(2,1)S(1)}, f32[257,128,128]{2,1,0:T(8,128)S(1)}) custom-call(bf16[16,128,128]{2,1,0:T(8,128)(2,1)S(1)} %get-tuple-element.13.base, bf16[16,128,128]{2,1,0:T(8,128)(2,1)S(1)} %collective-permute-done.beside, bf16[16,128,128]{2,1,0:T(8,128)(2,1)S(1)} %collective-permute-done.1.across, ...), custom_call_target="tpu_custom_call" | custom-call | flops 1073741824 | bytes 4194304 | tf_op jit(solution)/shard_map/half/pallas_call | solution.py:298
  33.3 0.0 collective-permute-done.6.high
  33.4 2.9 %last.1 = (f32[257,128,128]{2,1,0:T(8,128)S(1)}, bf16[64,128,128]{2,1,0:T(8,128)(2,1)}) custom-call(s32[2,10,64]{2,1,0:T(8,128)S(1)} %get-tuple-element.12.plan_in, bf16[16,128,128]{2,1,0:T(8,128)(2,1)S(1)} %get-tuple-element.15.panel, bf16[4,128,128]{2,1,0:T(8,128)(2,1)S(1)} %collective-permute-done.6.high, ...), custom_call_target="tpu_custom_call", output_to_operand_aliasing={{0}: (4, {})} | custom-call | flops 4294967296 | bytes 4194304 | tf_op jit(solution)/shard_map/last/pallas_call | solution.py:307
Async XLA Ops:
  1.3 3.1 %collective-permute-start = (bf16[16,128,128]{2,1,0:T(8,128)(2,1)S(1)}, bf16[16,128,128]{2,1,0:T(8,128)(2,1)S(1)}, u32[]{:S(2)}, u32[]{:S(2)}) collective-permute-start(bf16[16,128,128]{2,1,0:T(8,128)(2,1)S(1)} %get-tuple-element.13.base), channel_id=1, source_target_pairs={{0,1},{1,0},{2,3},{3,2},{4,5},{5,4},{6,7},{7,6},{8,9},{9,8},{10,11... | collective-permute-start | bytes 1572872 | tf_op jit(solution)/shard_map/ppermute | solution.py:243
  1.8 9.2 %collective-permute-start.1 = (bf16[16,128,128]{2,1,0:T(8,128)(2,1)S(1)}, bf16[16,128,128]{2,1,0:T(8,128)(2,1)S(1)}, u32[]{:S(2)}, u32[]{:S(2)}) collective-permute-start(bf16[16,128,128]{2,1,0:T(8,128)(2,1)S(1)} %get-tuple-element.13.base), channel_id=1, source_target_pairs={{0,2},{1,0},{2,3},{3,1},{4,5},{5,7},{6,4},{7,6},{8,9},{9,11},{10,8... | collective-permute-start | bytes 1572872 | tf_op jit(solution)/shard_map/ppermute | solution.py:243
  4.4 12.3 %collective-permute-start.3 = (bf16[16,128,128]{2,1,0:T(8,128)(2,1)S(1)}, bf16[16,128,128]{2,1,0:T(8,128)(2,1)S(1)}, u32[]{:S(2)}, u32[]{:S(2)}) collective-permute-start(bf16[16,128,128]{2,1,0:T(8,128)(2,1)S(1)} %collective-permute-done.beside), channel_id=1, source_target_pairs={{0,2},{1,0},{2,3},{3,1},{4,5},{5,4},{6,7},{7,6},{8,9},{9,11},{10,8... | collective-permute-start | bytes 1572872 | tf_op jit(solution)/shard_map/ppermute | solution.py:243
  11.1 11.7 %collective-permute-start.2 = (bf16[16,128,128]{2,1,0:T(8,128)(2,1)S(1)}, bf16[16,128,128]{2,1,0:T(8,128)(2,1)S(1)}, u32[]{:S(2)}, u32[]{:S(2)}) collective-permute-start(bf16[16,128,128]{2,1,0:T(8,128)(2,1)S(1)} %collective-permute-done.1.across), channel_id=1, source_target_pairs={{0,1},{1,0},{2,3},{3,2},{4,5},{5,4},{6,7},{7,6},{8,9},{9,8},{10,11... | collective-permute-start | bytes 1572872 | tf_op jit(solution)/shard_map/ppermute | solution.py:243
  16.7 14.8 %collective-permute-start.4 = (bf16[16,128,128]{2,1,0:T(8,128)(2,1)S(1)}, bf16[16,128,128]{2,1,0:T(8,128)(2,1)S(1)}, u32[]{:S(2)}, u32[]{:S(2)}) collective-permute-start(bf16[16,128,128]{2,1,0:T(8,128)(2,1)S(1)} %collective-permute-done.3.across1), channel_id=1, source_target_pairs={{0,1},{1,0},{2,3},{3,2},{4,5},{5,4},{6,7},{7,6},{8,9},{9,8},{10,11... | collective-permute-start | bytes 1572872 | tf_op jit(solution)/shard_map/ppermute | solution.py:243
  16.7 16.6 %collective-permute-start.6 = (bf16[4,128,128]{2,1,0:T(8,128)(2,1)S(1)}, bf16[4,128,128]{2,1,0:T(8,128)(2,1)S(1)}, u32[]{:S(2)}, u32[]{:S(2)}) collective-permute-start(bf16[4,128,128]{2,1,0:T(8,128)(2,1)S(1)} %get-tuple-element.16.high), channel_id=1, source_target_pairs={{0,28},{4,0},{8,4},{12,8},{16,12},{20,16},{24,20},{28,24},{1,29},{... | collective-permute-start | bytes 393224 | tf_op jit(solution)/shard_map/ppermute | solution.py:243
  16.7 14.8 %collective-permute-start.5 = (bf16[12,128,128]{2,1,0:T(8,128)(2,1)S(1)}, bf16[12,128,128]{2,1,0:T(8,128)(2,1)S(1)}, u32[]{:S(2)}, u32[]{:S(2)}) collective-permute-start(bf16[12,128,128]{2,1,0:T(8,128)(2,1)S(1)} %get-tuple-element.14.low), channel_id=1, source_target_pairs={{0,28},{4,0},{8,4},{12,8},{16,12},{20,16},{24,20},{28,24},{1,29},{... | collective-permute-start | bytes 1179656 | tf_op jit(solution)/shard_map/ppermute | solution.py:243

commit v2 on v1

v2 whole, which is shorter than its diff:
```python
import functools

import jax
import jax.numpy as jnp
from jax import lax
from jax.experimental import pallas as pl
from jax.experimental.pallas import tpu as pltpu
from jax.sharding import PartitionSpec as P


VMEM = pl.BlockSpec(memory_space=pltpu.VMEM)
HBM = pl.BlockSpec(memory_space=pltpu.HBM)


def in_vmem(x):
    return pltpu.with_memory_space_constraint(x, pltpu.VMEM)


def holders(row, col_count, ahead, bit):
    held = {(row + ahead) % col_count}
    step = col_count // 2
    while step > bit:
        held |= {c ^ step for c in held}
        step //= 2
    return held


def full_pairs(row_count, col_count, wanted):
    pairs = []
    for row in range(row_count):
        pair_of = dict(wanted(row))
        sources = [c for c in range(col_count) if c not in pair_of]
        targets = set(range(col_count)) - set(pair_of.values())
        for c in list(sources):
            if c ^ 1 in targets:
                pair_of[c] = c ^ 1
                targets.remove(c ^ 1)
                sources.remove(c)
        pair_of.update(zip(sources, sorted(targets)))
        pairs += [(row * col_count + c, row * col_count + to) for c, to in sorted(pair_of.items())]
    return pairs


def place():
    row, col = lax.axis_index("row"), lax.axis_index("col")
    return row % 2, (col ^ row) % 4, (col ^ (row + 1)) % 4


def plan_rows(index, dead):
    group, slots = index.shape
    rows = [index[g : g + 1] for g in range(group)]
    for turn in range(group):
        for g in range(turn % 2, group - 1, 2):
            rows[g], rows[g + 1] = jnp.minimum(*rows[g : g + 2]), jnp.maximum(*rows[g : g + 2])
    live = sum((row < dead).astype(jnp.float32) for row in rows)
    at_row = lax.broadcasted_iota(jnp.int32, (slots, slots), 0).astype(jnp.float32)
    at_col = lax.broadcasted_iota(jnp.int32, (slots, slots), 1).astype(jnp.float32)
    slot = at_col[:1]
    key = live * slots - slot
    column = jnp.sum(jnp.where(at_row == at_col, key, 0.0), axis=1, keepdims=True)
    rank = jnp.sum((key > column).astype(jnp.float32), axis=1, keepdims=True)
    pick = (rank == at_col).astype(jnp.float32)
    data = jnp.concatenate([row.astype(jnp.float32) for row in rows] + [live, slot], axis=0)
    sorted_data = jnp.dot(
        data, pick, precision=lax.Precision.HIGHEST, preferred_element_type=jnp.float32
    )
    return (sorted_data + 0.5).astype(jnp.int32)


def fetch_kernel(sizes, left, right, left_at, right_at, own, *rest):
    outs, (plan, at, sem) = rest[: len(sizes)], rest[len(sizes) :]
    row_count, col_count = lax.axis_size("row"), lax.axis_size("col")
    row = lax.axis_index("row")
    ahead = (row + lax.axis_index("col")) % 2
    slot = ((row + ahead) % row_count) // col_count
    stored = own.shape[0]
    pairs = [(left_at, at.at[0]), (right_at, at.at[1]), (left.at[slot], own)]
    for (source, first, count), out in zip(sizes, outs):
        origin = left.at[slot, pl.ds(first, count)] if source == 0 else right.at[pl.ds(first, count)]
        pairs.append((origin, out))
    copies = [pltpu.make_async_copy(x, y, sem.at[i]) for i, (x, y) in enumerate(pairs)]
    for copy in copies:
        copy.start()
    for copy in copies[:2]:
        copy.wait()
    dead = stored * stored
    index = jnp.where(at[0] < stored, at[1] * stored + at[0], dead)
    for step in range(plan.shape[0]):
        plan[step] = plan_rows(index[step], dead)
    for copy in copies[2:]:
        copy.wait()


def fetch(left_blocks, right_blocks, left_at, right_at, left_sizes, right_sizes):
    stored, *block = right_blocks.shape
    steps, group, slots = left_at.shape
    sizes = []
    for source, counts in ((0, left_sizes), (1, right_sizes)):
        first = 0
        for count in counts:
            sizes.append((source, first, count))
            first += count
    dtype = right_blocks.dtype
    outs = pl.pallas_call(
        functools.partial(fetch_kernel, tuple(sizes)),
        out_shape=(jax.ShapeDtypeStruct((stored, *block), dtype),)
        + tuple(jax.ShapeDtypeStruct((count, *block), dtype) for _, _, count in sizes)
        + (jax.ShapeDtypeStruct((steps, group + 2, slots), jnp.int32),),
        in_specs=[HBM] * 4,
        out_specs=(VMEM,) * (len(sizes) + 2),
        scratch_shapes=[
            pltpu.VMEM((2, steps, group, slots), jnp.int32),
            pltpu.SemaphoreType.DMA((len(sizes) + 3,)),
        ],
        compiler_params=pltpu.CompilerParams(vmem_limit_bytes=4 << 20),
        name="fetch",
    )(*(pltpu.with_memory_space_constraint(x, pltpu.HBM)
        for x in (left_blocks, right_blocks, left_at, right_at)))
    outs = [in_vmem(x) for x in outs]
    count = len(left_sizes)
    return outs[0], outs[1 : 1 + count], outs[1 + count : -1], outs[-1]


def cut_kernel(whole, *pieces):
    first = 0
    for piece in pieces:
        piece[...] = whole[pl.ds(first, piece.shape[0])]
        first += piece.shape[0]


def cut(whole, sizes):
    outs = pl.pallas_call(
        cut_kernel,
        out_shape=tuple(jax.ShapeDtypeStruct((n, *whole.shape[1:]), whole.dtype) for n in sizes),
        in_specs=[VMEM],
        out_specs=(VMEM,) * len(sizes),
        compiler_params=pltpu.CompilerParams(vmem_limit_bytes=4 << 20),
        name="cut",
    )(whole)
    return [in_vmem(x) for x in outs]


def merge_kernel(bit, base, received, out):
    row, col = lax.axis_index("row"), lax.axis_index("col")
    away = col ^ ((row + (row + col) % 2) % lax.axis_size("col"))
    take = (away & bit) != 0 if bit else row == lax.axis_size("row") - 1
    choose(out, [(take, received), (jnp.logical_not(take), base)])


def merge(bit, base, received):
    return in_vmem(pl.pallas_call(
        functools.partial(merge_kernel, bit),
        out_shape=jax.ShapeDtypeStruct(base.shape, base.dtype),
        in_specs=[VMEM, VMEM],
        out_specs=VMEM,
        compiler_params=pltpu.CompilerParams(vmem_limit_bytes=4 << 20),
        name="merge",
    )(in_vmem(base), in_vmem(received)))


def choose(panel, options):
    for condition, array in options:
        @pl.when(condition)
        def _():
            panel[...] = array[...]


def products(panel, right, out, first, span):
    stored, block, _ = panel.shape
    low, count = span
    rows = panel[pl.ds(low, count)].reshape(count * block, block)
    for q in range(right.shape[0] // 2):
        pair = jnp.concatenate([right[2 * q], right[2 * q + 1]], axis=1)
        x = jnp.dot(rows, pair, preferred_element_type=jnp.float32)
        base = (first + 2 * q) * stored + low
        out[pl.ds(base, count)] = x[:, :block].reshape(count, block, block)
        out[pl.ds(base + stored, count)] = x[:, block:].reshape(count, block, block)


def add_up(plan, step, table, per_turn, put):
    group = plan.shape[1] - 2

    def turn(i, carry):
        first = i * per_turn
        most = plan[step, group, first]

        def pick(low, high):
            if high - low == 1:
                for k in range(per_turn):
                    j = first + k
                    x = table[plan[step, 0, j]]
                    for g in range(1, low):
                        x = x + table[plan[step, g, j]]
                    put(plan[step, group + 1, j], x)
            else:
                middle = (low + high) // 2
                lax.cond(most < middle, lambda: pick(low, middle), lambda: pick(middle, high))

        pick(1, group + 1)
        return carry

    lax.fori_loop(0, plan.shape[2] // per_turn, turn, 0)


def clear_last(table):
    table[table.shape[0] - 1] = jnp.zeros(table.shape[1:], table.dtype)


def first_products_kernel(base, across, passed, beside0, beside1, right, panel, table):
    _, d0, _ = place()
    choose(panel, [(d0 == 0, base), (d0 == 2, across), (d0 == 3, passed)])

    @pl.when(d0 == 1)
    def _():
        low = beside0.shape[0]
        panel[pl.ds(0, low)] = beside0[...]
        panel[pl.ds(low, beside1.shape[0])] = beside1[...]

    products(panel, right, table, 0, (0, panel.shape[0]))
    clear_last(table)


def finish(plan_in, plan, sem, panel, right, table):
    planned = pltpu.make_async_copy(plan_in, plan, sem)
    planned.start()
    stored = panel.shape[0]
    products(panel, right, table, stored - right.shape[0], (0, stored))
    planned.wait()


def first_sums_kernel(per_turn, plan_in, panel, right, table_in, table, out, plan, sem):
    del table_in
    finish(plan_in, plan, sem, panel, right, table)

    def put(t, x):
        out[t] = x

    add_up(plan, 0, table, per_turn, put)


def choose_second(panel, span, base, beside, across, passed, across1, passed1):
    odd, d0, d1 = place()
    plain = odd == 1
    low, count = span
    part = pl.ds(low, count)
    choose(panel.at[part], [
        (d1 == 0, base.at[part]),
        (jnp.logical_and(d1 == 1, plain) | jnp.logical_and(d0 == 0, ~plain), beside),
        (jnp.logical_and(d1 == 2, plain), across.at[part]),
        (jnp.logical_and(d1 == 3, plain), passed.at[part]),
        (jnp.logical_and(d0 == 2, ~plain), across1),
        (jnp.logical_and(d0 == 3, ~plain), passed1),
    ])


def second_products_kernel(base, across, passed, beside, across1, passed1, right, panel, table):
    span = 0, beside.shape[0]
    choose_second(panel, span, base, beside, across, passed, across1, passed1)
    products(panel, right, table, 0, span)
    clear_last(table)


def middle_kernel(
    base, across, passed, beside, across1, passed1, right, panel_in, table_in, panel, table
):
    del panel_in, table_in
    span = panel.shape[0] - beside.shape[0], beside.shape[0]
    choose_second(panel, span, base, beside, across, passed, across1, passed1)
    products(panel, right, table, 0, span)


def last_kernel(per_turn, plan_in, panel, right, summed, table_in, table, out, stage, plan, sem):
    del table_in
    finish(plan_in, plan, sem.at[0], panel, right, table)

    def put(t, x):
        stage[t] = (summed[t] + x).astype(stage.dtype)
        pltpu.make_async_copy(stage.at[t], out.at[t], sem.at[1]).start()

    add_up(plan, 1, table, per_turn, put)
    pltpu.make_async_copy(stage, out, sem.at[1]).wait()


def cost(flops, bytes_accessed):
    return pl.CostEstimate(flops=flops, bytes_accessed=bytes_accessed, transcendentals=0)


def both_steps(left_blocks, right_blocks, left_index, right_index):
    row_count, col_count = lax.axis_size("row"), lax.axis_size("col")
    stored, block, _ = right_blocks.shape
    slots = left_index.shape[1]
    entries = stored * stored + 1
    both = ("row", "col")
    left_sizes = (stored - stored // 4, stored // 4)
    right_sizes = (stored - stored // 4, stored // 4)

    def permute(x, axis, pairs):
        return in_vmem(lax.ppermute(x, axis, pairs))

    left_at, right_at = left_index.transpose(0, 2, 1), right_index.transpose(0, 2, 1)
    base, pieces, rights, plan = fetch(
        left_blocks, right_blocks, left_at, right_at, left_sizes, right_sizes
    )
    bit = col_count // 2
    spread = bit > 2
    while bit > 2:
        pairs = full_pairs(row_count, col_count, lambda row: [
            (c, c ^ bit) for c in holders(row, col_count, 0, bit) | holders(row, col_count, 1, bit)
        ])
        base = merge(bit, base, lax.ppermute(base, both, pairs))
        bit //= 2
    if spread:
        pieces = cut(base, left_sizes)

    def crossing(rows, panels):
        return full_pairs(row_count, col_count, lambda row: [
            (c, c ^ 2)
            for ahead in range(panels(row))
            for c in holders(row, col_count, ahead, 2)
            if row in rows
        ])

    near = [(c, c ^ 1) for c in range(col_count)]
    down = [(r, (r - 1) % row_count) for r in range(row_count)]
    rows = range(row_count)
    cross = permute(base, both, crossing(rows[:-1], lambda row: 1 + row % 2))
    besides = [permute(x, "col", near) for x in pieces]
    moved = [permute(x, "row", down) for x in rights]
    last_cross = permute(base, both, crossing(rows[-1:], lambda row: 1 + row % 2))
    across1 = [permute(x, both, crossing(rows[::2], lambda row: 1)) for x in besides]
    across = merge(0, cross, last_cross)
    passed = permute(across, "col", near)
    passed1 = [permute(x, "col", near) for x in across1]

    per_turn = min(slots, 16)
    flops = 4 * stored * stored * block**3
    table_shape = jax.ShapeDtypeStruct((entries, block, block), jnp.float32)
    panel_shape = jax.ShapeDtypeStruct(base.shape, base.dtype)
    plan_scratch = pltpu.SMEM(plan.shape, plan.dtype)
    small = pltpu.CompilerParams(vmem_limit_bytes=6 << 20)
    panel, table = pl.pallas_call(
        first_products_kernel,
        out_shape=(panel_shape, table_shape),
        in_specs=[VMEM] * 6,
        out_specs=(VMEM, VMEM),
        compiler_params=small,
        cost_estimate=cost(flops, 4 << 20),
        name="products",
    )(base, across, passed, *besides, rights[0])
    _, summed = pl.pallas_call(
        functools.partial(first_sums_kernel, per_turn),
        out_shape=(table_shape, jax.ShapeDtypeStruct((slots, block, block), jnp.float32)),
        in_specs=[VMEM] * 4,
        out_specs=(VMEM, VMEM),
        scratch_shapes=[plan_scratch, pltpu.SemaphoreType.DMA],
        input_output_aliases={3: 0},
        compiler_params=small,
        cost_estimate=cost(flops, 4 << 20),
        name="sums",
    )(plan, in_vmem(panel), rights[1], in_vmem(table))
    panel, table = pl.pallas_call(
        second_products_kernel,
        out_shape=(panel_shape, table_shape),
        in_specs=[VMEM] * 7,
        out_specs=(VMEM, VMEM),
        compiler_params=small,
        cost_estimate=cost(flops // 2, 4 << 20),
        name="second",
    )(base, across, passed, besides[0], across1[0], passed1[0], moved[0])
    panel, table = pl.pallas_call(
        middle_kernel,
        out_shape=(panel_shape, table_shape),
        in_specs=[VMEM] * 9,
        out_specs=(VMEM, VMEM),
        input_output_aliases={7: 0, 8: 1},
        compiler_params=small,
        cost_estimate=cost(flops, 4 << 20),
        name="middle",
    )(
        base, across, passed, besides[1], across1[1], passed1[1], moved[0],
        in_vmem(panel), in_vmem(table),
    )
    return pl.pallas_call(
        functools.partial(last_kernel, per_turn),
        out_shape=(table_shape, jax.ShapeDtypeStruct((slots, block, block), jnp.bfloat16)),
        in_specs=[VMEM] * 5,
        out_specs=(VMEM, HBM),
        scratch_shapes=[
            pltpu.VMEM((slots, block, block), jnp.bfloat16),
            plan_scratch,
            pltpu.SemaphoreType.DMA((2,)),
        ],
        input_output_aliases={4: 0},
        compiler_params=small,
        cost_estimate=cost(2 * flops, 4 << 20),
        name="last",
    )(plan, in_vmem(panel), moved[1], in_vmem(summed), in_vmem(table))[1]


def solution(mesh):
    return jax.shard_map(
        both_steps,
        mesh=mesh,
        in_specs=(
            P(None, "row", "col", None),
            P("row", "col", None),
            P(None, "row", "col"),
            P(None, "row", "col"),
        ),
        out_specs=P("row", "col", None),
        check_vma=False,
    )
```

time: 36.4 us -> 33.4 us (0.918)
  waiting for transfers between devices: 14.7 us -> 11.7 us
  Pallas kernels: 10.4 us -> 9.85 us
  starting transfers between devices: 11 us -> 11.4 us
    ppermute x7 -> x11, waiting for transfers between devices: 14.7 us -> 11.7 us  [permute(): return in_vmem(lax.ppermute(x, axis, pairs))]
    ppermute x7 -> x11, starting transfers between devices: 11 us -> 11.4 us  [permute(): return in_vmem(lax.ppermute(x, axis, pairs))]
    pallas_call x3 -> x5, Pallas kernels: 5.45 us -> 5.33 us  [the longest x1 1.83 us: both_steps(): pl.pallas_call(first_products_kernel, out_shape=(panel_shape, table_shape...]
  transfers between devices with their start and end apart: 7 -> 11, of which waited for: 3 -> 4; matrix products, arithmetic and copies ran while one was open for 0% -> 0% of each run, Pallas kernels for 17% -> 17%
where the time goes in v2:
time: 33.4 us; the launch traced here: 33.1 us
  waiting for transfers between devices  11.7 us (35%)
  starting transfers between devices  11.4 us (34%)
  Pallas kernels  9.85 us (29%)
    ppermute x11, waiting for transfers between devices, permute(): return in_vmem(lax.ppermute(x, axis, pairs))  11.7 us
    ppermute x11, starting transfers between devices, permute(): return in_vmem(lax.ppermute(x, axis, pairs))  11.4 us
    pallas_call x1, Pallas kernels, both_steps(): pl.pallas_call(functools.partial(last_kernel, per_turn), out_shape=(table...  2.65 us
    pallas_call x1, Pallas kernels, both_steps(): pl.pallas_call(functools.partial(first_sums_kernel, per_turn), out_shape=...  1.87 us
    pallas_call x1, Pallas kernels, both_steps(): pl.pallas_call(first_products_kernel, out_shape=(panel_shape, table_shape...  1.83 us
    pallas_call x1, Pallas kernels, fetch(): pl.pallas_call(functools.partial(fetch_kernel, tuple(sizes)), out_shape=(...  1.46 us
    pallas_call x1, Pallas kernels, both_steps(): pl.pallas_call(second_products_kernel, out_shape=(panel_shape, table_shap...  1.41 us
  transfers between devices with their start and end apart: 11, of which 4 were waited for; matrix products, arithmetic and copies ran while one was open for 0% of the time, Pallas kernels for 17%

profile of v2, /device:TPU:0, one launch (start us, length us, event | category | flops | bytes accessed | tf_op | source)
XLA Modules:
  0.0 33.1 jit_solution(3930232296448781436)
XLA Ops:
  0.0 1.5 %fetch.1 = (bf16[16,128,128]{2,1,0:T(8,128)(2,1)S(1)}, bf16[12,128,128]{2,1,0:T(8,128)(2,1)S(1)}, bf16[4,128,128]{2,1,0:T(8,128)(2,1)S(1)}, bf16[12,128,128]{2,1...) custom-call(bf16[2,16,128,128]{3,2,1,0:T(8,128)(2,1)} %left.1, ...), custom_call_target="tpu_custom_call" | custom-call | tf_op jit(solution)/shard_map/fetch/pallas_call | solution.py:104
  1.5 3.0 %collective-permute-start = (bf16[16,128,128]{2,1,0:T(8,128)(2,1)S(1)}, bf16[16,128,128]{2,1,0:T(8,128)(2,1)S(1)}, u32[]{:S(2)}, u32[]{:S(2)}) collective-permute-start(bf16[16,128,128]{2,1,0:T(8,128)(2,1)S(1)} %get-tuple-element.20.base), channel_id=1, source_target_pairs={{0,2},{1,0},{2,3},{3,1},{4,5},{5,7},{6,4},{7,6},{8,9},{9,11},{10,8... | collective-permute-start | bytes 1572872 | tf_op jit(solution)/shard_map/ppermute | solution.py:298
  4.5 0.5 %collective-permute-start.7 = (bf16[12,128,128]{2,1,0:T(8,128)(2,1)S(1)}, bf16[12,128,128]{2,1,0:T(8,128)(2,1)S(1)}, u32[]{:S(2)}, u32[]{:S(2)}) collective-permute-start(bf16[12,128,128]{2,1,0:T(8,128)(2,1)S(1)} %get-tuple-element.23), channel_id=1, source_target_pairs={{0,1},{1,0},{2,3},{3,2},{4,5},{5,4},{6,7},{7,6},{8,9},{9,8},{10,11... | collective-permute-start | bytes 1179656 | tf_op jit(solution)/shard_map/ppermute | solution.py:298
  5.0 6.2 %collective-permute-done.base = bf16[16,128,128]{2,1,0:T(8,128)(2,1)S(1)} collective-permute-done((bf16[16,128,128]{2,1,0:T(8,128)(2,1)S(1)}, bf16[16,128,128]{2,1,0:T(8,128)(2,1)S(1)}, u32[]{:S(2)}, u32[]{:S(2)}) %collective-permute-start) | collective-permute-done | bytes 524320 | tf_op jit(solution)/shard_map/ppermute | solution.py:298
  11.2 0.1 collective-permute-start.2
  11.3 2.5 %collective-permute-start.8 = (bf16[12,128,128]{2,1,0:T(8,128)(2,1)S(1)}, bf16[12,128,128]{2,1,0:T(8,128)(2,1)S(1)}, u32[]{:S(2)}, u32[]{:S(2)}) collective-permute-start(bf16[12,128,128]{2,1,0:T(8,128)(2,1)S(1)} %collective-permute-done.7.beside.beside0), channel_id=1, source_target_pairs={{0,2},{1,0},{2,3},{3,1},{4,5},{5,4},{6,7},{7,6},{8,9},{9,11},{10,8... | collective-permute-start | bytes 1179656 | tf_op jit(solution)/shard_map/ppermute | solution.py:298
  13.9 0.0 collective-permute-start.3
  13.9 1.3 %collective-permute-done.3.beside.beside1 = bf16[4,128,128]{2,1,0:T(8,128)(2,1)S(1)} collective-permute-done((bf16[4,128,128]{2,1,0:T(8,128)(2,1)S(1)}, bf16[4,128,128]{2,1,0:T(8,128)(2,1)S(1)}, u32[]{:S(2)}, u32[]{:S(2)}) %collective-permute-start.3) | collective-permute-done | bytes 131104 | tf_op jit(solution)/shard_map/ppermute | solution.py:298
  15.2 0.9 %collective-permute-start.4 = (bf16[4,128,128]{2,1,0:T(8,128)(2,1)S(1)}, bf16[4,128,128]{2,1,0:T(8,128)(2,1)S(1)}, u32[]{:S(2)}, u32[]{:S(2)}) collective-permute-start(bf16[4,128,128]{2,1,0:T(8,128)(2,1)S(1)} %collective-permute-done.3.beside.beside1), channel_id=1, source_target_pairs={{0,2},{1,0},{2,3},{3,1},{4,5},{5,4},{6,7},{7,6},{8,9},{9,11},{10,8... | collective-permute-start | bytes 393224 | tf_op jit(solution)/shard_map/ppermute | solution.py:298
  16.1 2.8 %collective-permute-start.6 = (bf16[12,128,128]{2,1,0:T(8,128)(2,1)S(1)}, bf16[12,128,128]{2,1,0:T(8,128)(2,1)S(1)}, u32[]{:S(2)}, u32[]{:S(2)}) collective-permute-start(bf16[12,128,128]{2,1,0:T(8,128)(2,1)S(1)} %get-tuple-element.22.right), channel_id=1, source_target_pairs={{0,28},{4,0},{8,4},{12,8},{16,12},{20,16},{24,20},{28,24},{1,29},{... | collective-permute-start | bytes 1179656 | tf_op jit(solution)/shard_map/ppermute | solution.py:298
  18.9 1.1 %collective-permute-start.10 = (bf16[4,128,128]{2,1,0:T(8,128)(2,1)S(1)}, bf16[4,128,128]{2,1,0:T(8,128)(2,1)S(1)}, u32[]{:S(2)}, u32[]{:S(2)}) collective-permute-start(bf16[4,128,128]{2,1,0:T(8,128)(2,1)S(1)} %get-tuple-element.27.right), channel_id=1, source_target_pairs={{0,28},{4,0},{8,4},{12,8},{16,12},{20,16},{24,20},{28,24},{1,29},{... | collective-permute-start | bytes 393224 | tf_op jit(solution)/shard_map/ppermute | solution.py:298
  20.0 0.6 %collective-permute-done.4.across1 = bf16[4,128,128]{2,1,0:T(8,128)(2,1)S(1)} collective-permute-done((bf16[4,128,128]{2,1,0:T(8,128)(2,1)S(1)}, bf16[4,128,128]{2,1,0:T(8,128)(2,1)S(1)}, u32[]{:S(2)}, u32[]{:S(2)}) %collective-permute-start.4) | collective-permute-done | bytes 131104 | tf_op jit(solution)/shard_map/ppermute | solution.py:298
  20.6 0.3 collective-permute-start.5
  20.9 0.2 collective-permute-start.9
  21.1 0.0 collective-permute-done.2.passed
  21.1 1.8 %products.1 = (bf16[16,128,128]{2,1,0:T(8,128)(2,1)S(1)}, f32[257,128,128]{2,1,0:T(8,128)S(1)}) custom-call(bf16[16,128,128]{2,1,0:T(8,128)(2,1)S(1)} %get-tuple-element.20.base, bf16[16,128,128]{2,1,0:T(8,128)(2,1)S(1)} %merge.1.across, bf16[16,128,128]{2,1,0:T(8,128)(2,1)S(1)} %collective-permute-done.2.passed, ...), custom_call_target="tpu_custom_call" | custom-call | flops 2147483648 | bytes 4194304 | tf_op jit(solution)/shard_map/products/pallas_call | solution.py:341
  22.9 1.9 %sums.1 = (f32[257,128,128]{2,1,0:T(8,128)S(1)}, f32[64,128,128]{2,1,0:T(8,128)S(1)}) custom-call(s32[2,10,64]{2,1,0:T(8,128)S(1)} %get-tuple-element.19.plan_in, bf16[16,128,128]{2,1,0:T(8,128)(2,1)S(1)} %get-tuple-element.28.panel, bf16[4,128,128]{2,1,0:T(8,128)(2,1)S(1)} %get-tuple-element.27.right, ...), custom_call_target="tpu_custom_call", output_to_operand_aliasing={{0}: (3, {})} | custom-call | flops 2147483648 | bytes 4194304 | tf_op jit(solution)/shard_map/sums/pallas_call | solution.py:350
  24.8 3.6 %collective-permute-done.6.right = bf16[12,128,128]{2,1,0:T(8,128)(2,1)S(1)} collective-permute-done((bf16[12,128,128]{2,1,0:T(8,128)(2,1)S(1)}, bf16[12,128,128]{2,1,0:T(8,128)(2,1)S(1)}, u32[]{:S(2)}, u32[]{:S(2)}) %collective-permute-start.6) | collective-permute-done | bytes 393248 | tf_op jit(solution)/shard_map/ppermute | solution.py:298
  28.4 0.0 collective-permute-done.9.passed1
  28.4 1.4 %second.1 = (bf16[16,128,128]{2,1,0:T(8,128)(2,1)S(1)}, f32[257,128,128]{2,1,0:T(8,128)S(1)}) custom-call(bf16[16,128,128]{2,1,0:T(8,128)(2,1)S(1)} %get-tuple-element.20.base, bf16[16,128,128]{2,1,0:T(8,128)(2,1)S(1)} %merge.1.across, bf16[16,128,128]{2,1,0:T(8,128)(2,1)S(1)} %collective-permute-done.2.passed, ...), custom_call_target="tpu_custom_call" | custom-call | flops 1073741824 | bytes 4194304 | tf_op jit(solution)/shard_map/second/pallas_call | solution.py:361
  29.8 0.0 collective-permute-done.5.passed1
  29.8 0.6 %middle.1 = (bf16[16,128,128]{2,1,0:T(8,128)(2,1)S(1)}, f32[257,128,128]{2,1,0:T(8,128)S(1)}) custom-call(bf16[16,128,128]{2,1,0:T(8,128)(2,1)S(1)} %get-tuple-element.20.base, bf16[16,128,128]{2,1,0:T(8,128)(2,1)S(1)} %merge.1.across, bf16[16,128,128]{2,1,0:T(8,128)(2,1)S(1)} %collective-permute-done.2.passed, ...), custom_call_target="tpu_custom_call", output_to_operand_aliasing={{0}: (7, {}), {1}: (8, {})} | custom-call | flops 2147483648 | bytes 4194304 | tf_op jit(solution)/shard_map/middle/pallas_call | solution.py:370
  30.4 0.0 collective-permute-done.10.right
  30.5 2.7 %last.1 = (f32[257,128,128]{2,1,0:T(8,128)S(1)}, bf16[64,128,128]{2,1,0:T(8,128)(2,1)}) custom-call(s32[2,10,64]{2,1,0:T(8,128)S(1)} %get-tuple-element.19.plan_in, bf16[16,128,128]{2,1,0:T(8,128)(2,1)S(1)} %get-tuple-element.26.panel, bf16[4,128,128]{2,1,0:T(8,128)(2,1)S(1)} %collective-permute-done.10.right, ...), custom_call_target="tpu_custom_call", output_to_operand_aliasing={{0}: (4, {})} | custom-call | flops 4294967296 | bytes 4194304 | tf_op jit(solution)/shard_map/last/pallas_call | solution.py:383
  (5 shorter events, 0.0 us)
Async XLA Ops:
  1.5 9.7 %collective-permute-start = (bf16[16,128,128]{2,1,0:T(8,128)(2,1)S(1)}, bf16[16,128,128]{2,1,0:T(8,128)(2,1)S(1)}, u32[]{:S(2)}, u32[]{:S(2)}) collective-permute-start(bf16[16,128,128]{2,1,0:T(8,128)(2,1)S(1)} %get-tuple-element.20.base), channel_id=1, source_target_pairs={{0,2},{1,0},{2,3},{3,1},{4,5},{5,7},{6,4},{7,6},{8,9},{9,11},{10,8... | collective-permute-start | bytes 1572872 | tf_op jit(solution)/shard_map/ppermute | solution.py:298
  4.5 6.7 %collective-permute-start.1 = (bf16[16,128,128]{2,1,0:T(8,128)(2,1)S(1)}, bf16[16,128,128]{2,1,0:T(8,128)(2,1)S(1)}, u32[]{:S(2)}, u32[]{:S(2)}) collective-permute-start(bf16[16,128,128]{2,1,0:T(8,128)(2,1)S(1)} %get-tuple-element.20.base), channel_id=1, source_target_pairs={{0,1},{1,0},{2,3},{3,2},{4,5},{5,4},{6,7},{7,6},{8,9},{9,8},{10,11... | collective-permute-start | bytes 1572872 | tf_op jit(solution)/shard_map/ppermute | solution.py:298
  4.5 6.8 %collective-permute-start.7 = (bf16[12,128,128]{2,1,0:T(8,128)(2,1)S(1)}, bf16[12,128,128]{2,1,0:T(8,128)(2,1)S(1)}, u32[]{:S(2)}, u32[]{:S(2)}) collective-permute-start(bf16[12,128,128]{2,1,0:T(8,128)(2,1)S(1)} %get-tuple-element.23), channel_id=1, source_target_pairs={{0,1},{1,0},{2,3},{3,2},{4,5},{5,4},{6,7},{7,6},{8,9},{9,8},{10,11... | collective-permute-start | bytes 1179656 | tf_op jit(solution)/shard_map/ppermute | solution.py:298
  11.2 9.8 %collective-permute-start.2 = (bf16[16,128,128]{2,1,0:T(8,128)(2,1)S(1)}, bf16[16,128,128]{2,1,0:T(8,128)(2,1)S(1)}, u32[]{:S(2)}, u32[]{:S(2)}) collective-permute-start(bf16[16,128,128]{2,1,0:T(8,128)(2,1)S(1)} %merge.1.across), channel_id=1, source_target_pairs={{0,1},{1,0},{2,3},{3,2},{4,5},{5,4},{6,7},{7,6},{8,9},{9,8},{10,11... | collective-permute-start | bytes 1572872 | tf_op jit(solution)/shard_map/ppermute | solution.py:298
  11.3 9.6 %collective-permute-start.8 = (bf16[12,128,128]{2,1,0:T(8,128)(2,1)S(1)}, bf16[12,128,128]{2,1,0:T(8,128)(2,1)S(1)}, u32[]{:S(2)}, u32[]{:S(2)}) collective-permute-start(bf16[12,128,128]{2,1,0:T(8,128)(2,1)S(1)} %collective-permute-done.7.beside.beside0), channel_id=1, source_target_pairs={{0,2},{1,0},{2,3},{3,1},{4,5},{5,4},{6,7},{7,6},{8,9},{9,11},{10,8... | collective-permute-start | bytes 1179656 | tf_op jit(solution)/shard_map/ppermute | solution.py:298
  13.9 1.3 %collective-permute-start.3 = (bf16[4,128,128]{2,1,0:T(8,128)(2,1)S(1)}, bf16[4,128,128]{2,1,0:T(8,128)(2,1)S(1)}, u32[]{:S(2)}, u32[]{:S(2)}) collective-permute-start(bf16[4,128,128]{2,1,0:T(8,128)(2,1)S(1)} %get-tuple-element.21), channel_id=1, source_target_pairs={{0,1},{1,0},{2,3},{3,2},{4,5},{5,4},{6,7},{7,6},{8,9},{9,8},{10,11... | collective-permute-start | bytes 393224 | tf_op jit(solution)/shard_map/ppermute | solution.py:298
  15.2 5.4 %collective-permute-start.4 = (bf16[4,128,128]{2,1,0:T(8,128)(2,1)S(1)}, bf16[4,128,128]{2,1,0:T(8,128)(2,1)S(1)}, u32[]{:S(2)}, u32[]{:S(2)}) collective-permute-start(bf16[4,128,128]{2,1,0:T(8,128)(2,1)S(1)} %collective-permute-done.3.beside.beside1), channel_id=1, source_target_pairs={{0,2},{1,0},{2,3},{3,1},{4,5},{5,4},{6,7},{7,6},{8,9},{9,11},{10,8... | collective-permute-start | bytes 393224 | tf_op jit(solution)/shard_map/ppermute | solution.py:298
  16.1 12.3 %collective-permute-start.6 = (bf16[12,128,128]{2,1,0:T(8,128)(2,1)S(1)}, bf16[12,128,128]{2,1,0:T(8,128)(2,1)S(1)}, u32[]{:S(2)}, u32[]{:S(2)}) collective-permute-start(bf16[12,128,128]{2,1,0:T(8,128)(2,1)S(1)} %get-tuple-element.22.right), channel_id=1, source_target_pairs={{0,28},{4,0},{8,4},{12,8},{16,12},{20,16},{24,20},{28,24},{1,29},{... | collective-permute-start | bytes 1179656 | tf_op jit(solution)/shard_map/ppermute | solution.py:298
  18.9 11.6 %collective-permute-start.10 = (bf16[4,128,128]{2,1,0:T(8,128)(2,1)S(1)}, bf16[4,128,128]{2,1,0:T(8,128)(2,1)S(1)}, u32[]{:S(2)}, u32[]{:S(2)}) collective-permute-start(bf16[4,128,128]{2,1,0:T(8,128)(2,1)S(1)} %get-tuple-element.27.right), channel_id=1, source_target_pairs={{0,28},{4,0},{8,4},{12,8},{16,12},{20,16},{24,20},{28,24},{1,29},{... | collective-permute-start | bytes 393224 | tf_op jit(solution)/shard_map/ppermute | solution.py:298
  20.6 9.2 %collective-permute-start.5 = (bf16[4,128,128]{2,1,0:T(8,128)(2,1)S(1)}, bf16[4,128,128]{2,1,0:T(8,128)(2,1)S(1)}, u32[]{:S(2)}, u32[]{:S(2)}) collective-permute-start(bf16[4,128,128]{2,1,0:T(8,128)(2,1)S(1)} %collective-permute-done.4.across1), channel_id=1, source_target_pairs={{0,1},{1,0},{2,3},{3,2},{4,5},{5,4},{6,7},{7,6},{8,9},{9,8},{10,11... | collective-permute-start | bytes 393224 | tf_op jit(solution)/shard_map/ppermute | solution.py:298
  20.9 7.5 %collective-permute-start.9 = (bf16[12,128,128]{2,1,0:T(8,128)(2,1)S(1)}, bf16[12,128,128]{2,1,0:T(8,128)(2,1)S(1)}, u32[]{:S(2)}, u32[]{:S(2)}) collective-permute-start(bf16[12,128,128]{2,1,0:T(8,128)(2,1)S(1)} %collective-permute-done.8.across1), channel_id=1, source_target_pairs={{0,1},{1,0},{2,3},{3,2},{4,5},{5,4},{6,7},{7,6},{8,9},{9,8},{10,11... | collective-permute-start | bytes 1179656 | tf_op jit(solution)/shard_map/ppermute | solution.py:298
